TPU v7x, 256 devices: a whole 4x4x8 slice. The times are simulated.
256 devices in a mesh: space: 32 (over y, x, core), slot: 8 (over z).
Axes of the slice: x: 4, y: 4, z: 8, core: 2. Of those that a mesh axis runs over, the one named last changes fastest.
Arguments:
- window_values: bfloat16 [65536, 16384], P('space', 'slot'), may hold values from -4 to 4
- window_scales: bfloat16 [512, 16384], P('space', 'slot'), may hold values from 0.049804688 to 1
- slab_values: bfloat16 [65536, 512], P('space', 'slot'), may hold values from -4 to 4
- slab_scales: bfloat16 [512, 512], P('space', 'slot'), may hold values from 0.049804688 to 1
- test_matrix: bfloat16 [16384, 256], P('slot'), may hold values from -1 to 1
- owner_slot: int32 [8], replicated, may hold values from 0 to 7, each once
- offset: int32 [1], replicated, may hold values from 0 to 1536
Outputs:
- pod_basis: bfloat16 [65536, 256], P('space')
- pod_coefs: float32 [256, 16384], P(None, 'slot')
All inputs are finite; a program needn't handle non-finite values.
Results may differ from a plain program's by a relative error of at most 0.0049.
Values may be sent and summed in bfloat16 or wider, within the bound.
No kernel may reach another device: no remote copies, remote signals or barrier semaphores. Data moves between devices by JAX's collectives and lax.ppermute only.
A program may use at most 128 MiB of HBM per device.

v0:
```python
import functools

import jax
import jax.numpy as jnp
from jax import lax
from jax.experimental import pallas as pl
from jax.experimental.pallas import tpu as pltpu
from jax.sharding import PartitionSpec as P


SLAB = 512
BLOCK = 128
F32, BF16 = jnp.float32, jnp.bfloat16
HIGHEST = lax.Precision.HIGHEST

CORES = 2


def space_shift(dy, dx, dc=0):
    index = lambda y, x, c: (y % 4) * 8 + (x % 4) * 2 + c
    return [
        (index(y, x, c), index(y + dy, x + dx, (c + dc) % 2))
        for y in range(4)
        for x in range(4)
        for c in range(2)
    ]


def ring(value, distance, size):
    return lax.ppermute(value, "slot", [(i, (i + distance) % size) for i in range(size)])


def along(value, dy, dx, dc=0):
    return lax.ppermute(value, "space", space_shift(dy, dx, dc))


def contract(left, right, left_dim, right_dim, precision=None):
    return lax.dot_general(
        left,
        right,
        (((left_dim,), (right_dim,)), ((), ())),
        precision=precision,
        preferred_element_type=F32,
    )


def split(value):
    high = value.astype(BF16)
    return high, (value - high.astype(F32)).astype(BF16)


VMEM = pl.BlockSpec(memory_space=pltpu.VMEM)
SMEM = pl.BlockSpec(memory_space=pltpu.SMEM)


def expand(values_ref, scale_ref, first, count):
    return jnp.concatenate(
        [
            values_ref[BLOCK * b : BLOCK * (b + 1), :] * scale_ref[b : b + 1, :].astype(BF16)
            for b in range(first, first + count)
        ],
        axis=0,
    )


def expand_slab(slab_ref, scale_ref, row_blocks):
    return jnp.concatenate(
        [
            slab_ref[:, BLOCK * b : BLOCK * (b + 1)] * scale_ref[:, b : b + 1].astype(BF16)
            for b in range(row_blocks)
        ],
        axis=1,
    )


def sketch_kernel(meta, values_ref, scales_ref, test_ref, out_ref, scale_ref):
    columns = lax.broadcasted_iota(jnp.int32, scales_ref.shape, 1)
    evicted = (columns >= meta[2]) & (columns < meta[2] + SLAB)
    scale_ref[...] = jnp.where(evicted, 0.0, scales_ref[...].astype(F32))
    row_blocks = scales_ref.shape[0]
    count = row_blocks // 4
    for first in range(0, row_blocks, count):
        window = expand(values_ref, scale_ref, first, count)
        out_ref[BLOCK * first : BLOCK * (first + count), :] = jnp.dot(
            window, test_ref[...], preferred_element_type=F32
        )


def sketch_window(meta, values, scales, test):
    return pl.pallas_call(
        sketch_kernel,
        in_specs=[SMEM] + [VMEM] * 3,
        out_specs=VMEM,
        out_shape=jax.ShapeDtypeStruct((values.shape[0], test.shape[1]), F32),
        scratch_shapes=[pltpu.VMEM(scales.shape, F32)],
        compiler_params=pltpu.CompilerParams(vmem_limit_bytes=40 * 2**20),
        name="sketch_window",
    )(meta, values, scales, test)


def slab_kernel(parts, meta, partial_ref, slab_ref, scales_ref, tests_ref, *refs):
    out_refs, sum_ref, scale_ref = refs[:-2], refs[-2], refs[-1]
    rows = partial_ref.shape[0] // parts
    scale_ref[...] = scales_ref[...].astype(F32)
    slab = expand_slab(slab_ref, scale_ref, partial_ref.shape[0] // BLOCK)
    sum_ref[...] = (partial_ref[...] + contract(slab, tests_ref[meta[3]], 0, 0)).astype(BF16)
    pieces = []
    for k in range(parts):
        whole = (k, 0, rows)
        pieces += [(k, 0, rows // 2), (k, rows // 2, rows)] if 2 * k == parts else [whole]
    for out_ref, (k, start, stop) in zip(out_refs, pieces):
        block = pl.multiple_of(lax.rem(meta[0] + k, parts) * rows + start, rows // 2)
        out_ref[...] = sum_ref[pl.ds(block, stop - start), :]


def add_slab(meta, partial, slab, scales, tests, parts):
    rows, rank = partial.shape
    sizes = [rows // parts] * (parts // 2) + [rows // parts // 2] * 2
    sizes += [rows // parts] * (parts // 2 - 1)
    return pl.pallas_call(
        functools.partial(slab_kernel, parts),
        in_specs=[SMEM] + [VMEM] * 4,
        out_specs=[VMEM] * len(sizes),
        out_shape=[jax.ShapeDtypeStruct((size, rank), BF16) for size in sizes],
        scratch_shapes=[pltpu.VMEM(partial.shape, BF16), pltpu.VMEM(scales.shape, F32)],
        compiler_params=pltpu.CompilerParams(vmem_limit_bytes=40 * 2**20),
        name="add_slab",
    )(meta, partial, slab, scales, tests)


def gather_blocks(parts, meta, sketch_refs, out_ref):
    rows = out_ref.shape[0] // parts
    start = 0
    for ref in sketch_refs:
        k, inside = divmod(start, rows)
        line = pl.multiple_of(lax.rem(meta[0] + k, parts) * rows + inside, rows // 2)
        out_ref[pl.ds(line, ref.shape[0]), :] = ref[...]
        start += ref.shape[0]


def cross_kernel(parts, meta, values_ref, scales_ref, slab_ref, slab_scales_ref, *refs):
    sketch_refs, refs = refs[:-9], refs[-9:]
    mine_ref, theirs_ref, gram_mine_ref, gram_theirs_ref, sketch_ref = refs[:5]
    cross_ref, gram_ref, scale_ref, slab_scale_ref = refs[5:]
    gather_blocks(parts, meta, sketch_refs, sketch_ref)
    scale_ref[...] = scales_ref[...].astype(F32)
    slab_scale_ref[...] = slab_scales_ref[...].astype(F32)
    rank, row_blocks = sketch_ref.shape[1], scales_ref.shape[0]
    width, cols = slab_ref.shape[0], values_ref.shape[1]
    sketch = sketch_ref[...]
    gram = contract(sketch, sketch, 0, 0)
    half, eighth = rank // 2, rank // 8
    for c in range(CORES):
        block = gram[half * c : half * (c + 1), half * c : half * (c + 1)]
        below = gram[half + 2 * eighth * c : half + 2 * eighth * (c + 1), :half]
        gram_ref[c, : half // 2, :half] = block[: half // 2]
        gram_ref[c, : half // 2, half:] = block[half // 2 :]
        gram_ref[c, half // 2 :, :half] = below[:eighth]
        gram_ref[c, half // 2 :, half:] = below[eighth:]
    slab = expand_slab(slab_ref, slab_scale_ref, row_blocks)
    cross_ref[:, cols:] = jnp.zeros((rank, cross_ref.shape[1] - cols), F32)
    cross_ref[:, cols : cols + width] = contract(sketch, slab, 0, 1)
    count = row_blocks // 2
    for first in range(0, row_blocks, count):
        window = expand(values_ref, scale_ref, first, count)
        part = contract(sketch[BLOCK * first : BLOCK * (first + count), :], window, 0, 0)
        cross_ref[:, :cols] = part if first == 0 else cross_ref[:, :cols] + part
    core = meta[1]
    for out, gram_out, which in (
        (mine_ref, gram_mine_ref, core),
        (theirs_ref, gram_theirs_ref, 1 - core),
    ):
        lines = pl.ds(pl.multiple_of(which * half, half), half)
        out[...] = cross_ref[lines, :].astype(BF16)
        gram_out[...] = gram_ref[which]


def products(meta, values, scales, slab, slab_scales, sketch_blocks, parts):
    rows, cols = values.shape
    rank = sketch_blocks[0].shape[1]
    half, lanes = rank // CORES, cols + 128
    gram_half = (3 * rank // 8, rank)
    return pl.pallas_call(
        functools.partial(cross_kernel, parts),
        in_specs=[SMEM] + [VMEM] * (4 + len(sketch_blocks)),
        out_specs=[VMEM] * 5,
        out_shape=[jax.ShapeDtypeStruct((half, lanes), BF16)] * 2
        + [jax.ShapeDtypeStruct(gram_half, F32)] * 2
        + [jax.ShapeDtypeStruct((rows, rank), BF16)],
        scratch_shapes=[
            pltpu.VMEM((rank, lanes), F32),
            pltpu.VMEM((CORES, *gram_half), F32),
            pltpu.VMEM(scales.shape, F32),
            pltpu.VMEM(slab_scales.shape, F32),
        ],
        compiler_params=pltpu.CompilerParams(vmem_limit_bytes=40 * 2**20),
        name="products",
    )(meta, values, scales, slab, slab_scales, *sketch_blocks)


def pair_kernel(mine_ref, other_ref, out_ref):
    lines = out_ref.shape[1]
    total = mine_ref[...].astype(F32) + other_ref[...].astype(F32)
    for chip in range(out_ref.shape[0]):
        out_ref[chip] = total[lines * chip : lines * (chip + 1), :].astype(BF16)


def add_pair(mine, other, chips):
    rows, lanes = mine.shape
    return pl.pallas_call(
        pair_kernel,
        in_specs=[VMEM] * 2,
        out_specs=VMEM,
        out_shape=jax.ShapeDtypeStruct((chips, rows // chips, lanes), BF16),
        compiler_params=pltpu.CompilerParams(vmem_limit_bytes=40 * 2**20),
        name="add_pair",
    )(mine, other)


def sum_kernel(pieces_ref, cross_ref, new_ref):
    cols = cross_ref.shape[1]
    total = pieces_ref[0].astype(F32)
    for chip in range(1, pieces_ref.shape[0]):
        total += pieces_ref[chip].astype(F32)
    cross_ref[...] = total[:, :cols]
    new = total[:, cols:].astype(BF16)
    for slot in range(new_ref.shape[0]):
        new_ref[slot] = new


def sum_pieces(pieces, cols, slots):
    _, lines, lanes = pieces.shape
    return pl.pallas_call(
        sum_kernel,
        in_specs=[VMEM],
        out_specs=[VMEM] * 2,
        out_shape=[
            jax.ShapeDtypeStruct((lines, cols), F32),
            jax.ShapeDtypeStruct((slots, lines, lanes - cols), BF16),
        ],
        compiler_params=pltpu.CompilerParams(vmem_limit_bytes=40 * 2**20),
        name="sum_pieces",
    )(pieces)


def insert_kernel(width, meta, cross_ref, slabs_ref, out_ref, line_ref):
    lines, cols = cross_ref.shape
    line_ref[:, :cols] = cross_ref[...]

    @pl.when(meta[2] < cols)
    def _():
        slots, _, lanes = slabs_ref.shape
        inside = lax.rem(meta[2], 128)
        window = pl.ds(pl.multiple_of(meta[2] - inside, 128), SLAB + 128)
        column = lax.broadcasted_iota(jnp.int32, (lanes, SLAB + 128), 1)
        row = lax.broadcasted_iota(jnp.int32, (lanes, SLAB + 128), 0)
        placed = jnp.zeros((lines, SLAB + 128), F32)
        for slot in range(slots):
            hit = (column == row + (inside + width * slot)) & (row < width)
            selection = jnp.where(hit, 1.0, 0.0).astype(BF16)
            placed += contract(slabs_ref[slot], selection, 1, 0)
        column = lax.broadcasted_iota(jnp.int32, placed.shape, 1)
        replaced = (column >= inside) & (column < inside + SLAB)
        line_ref[:, window] = jnp.where(replaced, placed, line_ref[:, window])

    cross = line_ref[:, :cols].astype(BF16)
    for chip in range(out_ref.shape[0]):
        out_ref[chip] = cross


def insert(meta, cross, slabs, width, chips):
    lines, cols = cross.shape
    return pl.pallas_call(
        functools.partial(insert_kernel, width),
        in_specs=[SMEM] + [VMEM] * 2,
        out_specs=VMEM,
        out_shape=jax.ShapeDtypeStruct((chips, lines, cols), BF16),
        scratch_shapes=[pltpu.VMEM((lines, cols + 128), F32)],
        compiler_params=pltpu.CompilerParams(vmem_limit_bytes=40 * 2**20),
        name="insert",
    )(meta, cross, slabs)


def sublane(value, row):
    return jnp.broadcast_to(value[row : row + 1, :], value.shape)


def lane(value, col):
    return jnp.broadcast_to(value[:, col : col + 1], value.shape)


def inverse_factor(matrix):
    size = matrix.shape[0]
    groups = size // 8
    cols = lax.broadcasted_iota(jnp.int32, (8, size), 1)
    rows = lax.broadcasted_iota(jnp.int32, (8, size), 0)
    a = [matrix[8 * g : 8 * g + 8, :] for g in range(groups)]
    m = [jnp.where(cols == rows + 8 * g, 1.0, 0.0).astype(F32) for g in range(groups)]
    for g in range(groups):
        pivot = [lane(a[g], 8 * g + c) for c in range(8)]
        below = {h: [lane(a[h], 8 * g + c) for c in range(8)] for h in range(g + 1, groups)}
        for c in range(8):
            reciprocal = 1.0 / sublane(pivot[c], c)
            a_row, m_row = sublane(a[g], c), sublane(m[g], c)
            pivots = [sublane(pivot[k], c) for k in range(8)]
            if c < 7:
                factor = jnp.where(rows > c, pivot[c] * reciprocal, 0.0)
                a[g] = a[g] - factor * a_row
                m[g] = m[g] - factor * m_row
                for k in range(c + 1, 8):
                    pivot[k] = pivot[k] - factor * pivots[k]
            for h in range(g + 1, groups):
                factor = below[h][c] * reciprocal
                a[h] = a[h] - factor * a_row
                m[h] = m[h] - factor * m_row
                for k in range(c + 1, 8):
                    below[h][k] = below[h][k] - factor * pivots[k]
    out = []
    for g in range(groups):
        diagonal = jnp.sum(jnp.where(cols == rows + 8 * g, a[g], 0.0), axis=1, keepdims=True)
        out.append(m[g] * lax.rsqrt(diagonal))
    return jnp.concatenate(out, axis=0)


def factor_kernel(row_total, meta, mine_ref, other_ref, out_ref, gram_ref):
    half = out_ref.shape[0] // 2
    eighth = half // 4
    gram_ref[meta[1]] = mine_ref[...]
    gram_ref[1 - meta[1]] = other_ref[...]
    gram = gram_ref[...] * (1.0 / row_total)
    unpack = lambda rows: jnp.concatenate([rows[:, :half], rows[:, half:]], axis=0)
    lower = jnp.concatenate([unpack(gram[0, 2 * eighth :]), unpack(gram[1, 2 * eighth :])], axis=0)
    first = inverse_factor(unpack(gram[0, : 2 * eighth]))
    upper = contract(first, lower, 1, 1, HIGHEST)
    rest = unpack(gram[1, : 2 * eighth]) - contract(upper, upper, 0, 0, HIGHEST)
    below = -contract(upper, first, 0, 0, HIGHEST)
    second = inverse_factor(rest)
    out_ref[:half, :half] = first
    out_ref[:half, half:] = jnp.zeros((half, half), F32)
    out_ref[half:, :half] = contract(second, below, 1, 0, HIGHEST)
    out_ref[half:, half:] = second


def invert(meta, mine, other, row_total):
    rank = mine.shape[1]
    return pl.pallas_call(
        functools.partial(factor_kernel, row_total),
        in_specs=[SMEM, VMEM, VMEM],
        out_specs=VMEM,
        out_shape=jax.ShapeDtypeStruct((rank, rank), F32),
        scratch_shapes=[pltpu.VMEM((CORES, *mine.shape), F32)],
        compiler_params=pltpu.CompilerParams(vmem_limit_bytes=40 * 2**20),
        name="invert",
    )(meta, mine, other)


def basis_kernel(inverse_ref, sketch_ref, out_ref):
    high, low = split(inverse_ref[...])
    sketch = sketch_ref[...]
    out_ref[...] = (contract(sketch, high, 1, 1) + contract(sketch, low, 1, 1)).astype(BF16)


def basis(inverse, sketch):
    return pl.pallas_call(
        basis_kernel,
        in_specs=[VMEM] * 2,
        out_specs=VMEM,
        out_shape=jax.ShapeDtypeStruct(sketch.shape, BF16),
        compiler_params=pltpu.CompilerParams(vmem_limit_bytes=40 * 2**20),
        name="basis",
    )(inverse, sketch)


def coefs_kernel(scale, meta, inverse_ref, mine_ref, other_ref, out_ref, cross_ref):
    half, _ = mine_ref.shape
    for ref, core in ((mine_ref, meta[1]), (other_ref, 1 - meta[1])):
        cross_ref[pl.ds(pl.multiple_of(core * half, half), half), :] = ref[...]
    high, low = split(inverse_ref[...] * scale)
    cross = cross_ref[...]
    out_ref[...] = contract(high, cross, 1, 0) + contract(low, cross, 1, 0)


def coefs(meta, inverse, mine, other, scale):
    rank, cols = inverse.shape[0], mine.shape[1]
    return pl.pallas_call(
        functools.partial(coefs_kernel, scale),
        in_specs=[SMEM] + [VMEM] * 3,
        out_specs=VMEM,
        out_shape=jax.ShapeDtypeStruct((rank, cols), F32),
        scratch_shapes=[pltpu.VMEM((rank, cols), BF16)],
        compiler_params=pltpu.CompilerParams(vmem_limit_bytes=40 * 2**20),
        name="coefs",
    )(meta, inverse, mine, other)


def exchange(value, axis, groups=None):
    return lax.all_to_all(value, axis, 0, 0, axis_index_groups=groups, tiled=True)


def local(window_values, window_scales, slab_values, slab_scales, test_matrix, owner_slot, offset):
    rows, cols = window_values.shape
    rank = test_matrix.shape[1]
    width = slab_values.shape[1]
    slots, spaces = lax.axis_size("slot"), lax.axis_size("space")
    chips = spaces // CORES
    same_core = [[CORES * i + c for i in range(chips)] for c in range(CORES)]
    row_total = rows * spaces
    slot, core = lax.axis_index("slot"), lax.rem(lax.axis_index("space"), CORES)
    owner, first = owner_slot[0], offset[0]
    where = jnp.arange(4)
    meta = jnp.where(
        where == 0,
        slot,
        jnp.where(
            where == 1,
            core,
            jnp.where(where == 2, jnp.where(slot == owner, first, 2 * cols), owner),
        ),
    ).astype(jnp.int32)

    test_rows = lax.dynamic_slice_in_dim(test_matrix, first, SLAB, 0)
    tests = lax.all_to_all(test_rows.reshape(slots, width, rank), "slot", 0, 0, tiled=True)
    window_values = pltpu.with_memory_space_constraint(window_values, pltpu.VMEM)
    partial = sketch_window(meta, window_values, window_scales, test_matrix)
    slab, slab_scale = slab_values.T, slab_scales.T
    x0, x1, x2, x3, x4a, x4b, x5, x6, x7 = add_slab(
        meta, partial, slab, slab_scale, tests, slots
    )

    right3, left3 = ring(x3, 1, slots), ring(x5, -1, slots)
    right4, left4 = ring(x4a, 2, slots), ring(x4b, -2, slots)
    right1, left1 = ring(x1, 1, slots), ring(x7, -1, slots)
    upper = x4a.shape[0]
    wide = lambda x: x.astype(F32)
    to_right = wide(x2) + wide(right3) + jnp.pad(wide(right4), ((0, upper), (0, 0)))
    to_left = wide(x6) + wide(left3) + jnp.pad(wide(left4), ((upper, 0), (0, 0)))
    right2, left2 = ring(to_right.astype(BF16), 2, slots), ring(to_left.astype(BF16), -2, slots)
    own = (wide(x0) + wide(right1) + wide(left1) + wide(right2) + wide(left2)).astype(BF16)

    right2, left2 = ring(own, 2, slots), ring(own, -2, slots)
    right1, left1 = ring(own, 1, slots), ring(own, -1, slots)
    right3, left3 = ring(right2, 1, slots), ring(left2, -1, slots)
    right4, left4 = ring(right2[:upper], 2, slots), ring(left2[upper:], -2, slots)
    sketch_blocks = [own, left1, left2, left3, right4, left4, right3, right2, right1]

    mine, theirs, gram_mine, gram_theirs, sketch = products(
        meta, window_values, window_scales, slab, slab_scale, sketch_blocks, slots
    )

    half = add_pair(mine, along(theirs, 0, 0, 1), chips)
    pieces = exchange(half, "space", same_core)
    total, new = sum_pieces(pieces, cols, slots)
    slabs = exchange(new, "slot")
    whole = insert(meta, total, slabs, width, chips)
    cross_mine = exchange(whole, "space", same_core)
    cross_mine = cross_mine.reshape(rank // CORES, cols)
    cross_other = along(cross_mine, 0, 0, 1)

    gram = gram_mine + along(gram_theirs, 0, 0, 1)
    for dy, dx in ((0, 1), (1, 0)):
        far, near, back = (along(gram, dy * d, dx * d) for d in (2, 1, 3))
        gram = (gram + far) + (near + back)
    gram_other = along(gram, 0, 0, 1)

    inverse = invert(meta, gram, gram_other, row_total)
    pod_basis = basis(inverse, sketch)
    pod_coefs = coefs(meta, inverse, cross_mine, cross_other, 1.0 / float(row_total) ** 0.5)
    return pod_basis, pod_coefs


def solution(mesh):
    return jax.shard_map(
        local,
        mesh=mesh,
        in_specs=(
            P("space", "slot"),
            P("space", "slot"),
            P("space", "slot"),
            P("space", "slot"),
            P("slot", None),
            P(),
            P(),
        ),
        out_specs=(P("space", None), P(None, "slot")),
        check_vma=False,
    )
```

profile of v0, /device:TPU:1, one launch (start us, length us, event | category | flops | bytes accessed | tf_op | source)
XLA Modules:
  0.0 156.8 jit_solution(3592889734184156626)
XLA Ops:
  3.0 9.0 %all-to-all-start = ((bf16[8,64,256]{2,1,0:T(8,128)(2,1)}), bf16[8,64,256]{2,1,0:T(8,128)(2,1)S(1)}, u32[]{:S(2)}, u32[]{:S(2)}) async-start(bf16[8,64,256]{2,1,0:T(8,128)(2,1)} %bitcast.4), calls=%async_computation | async-start | bytes 524288 | tf_op jit(solution)/shard_map/all_to_all | solution.py:422
  14.1 3.4 %copy-done = bf16[2048,2048]{1,0:T(8,128)(2,1)S(1)} copy-done((bf16[2048,2048]{1,0:T(8,128)(2,1)S(1)}, bf16[2048,2048]{1,0:T(8,128)(2,1)}, u32[]{:S(2)}) %copy-start) | copy-done | bytes 8388632
  19.6 2.9 %sketch_window.1.partial_ref = f32[2048,256]{1,0:T(8,128)S(1)} custom-call(s32[4]{0:T(128)S(1)} %compare_select_fusion.2.meta, bf16[2048,2048]{1,0:T(8,128)(2,1)S(1)} %copy-done, bf16[16,2048]{1,0:T(8,128)(2,1)S(1)} %copy-done.4, bf16[2048,256]{1,0:T(8,128)(2,1)S(1)} %copy-done.2), custom_call_target="tpu_custom_call" | custom-call | tf_op jit(solution)/shard_map/sketch_window/pallas_call | solution.py:90
  25.4 2.1 %collective-permute-start.3 = (bf16[128,256]{1,0:T(8,128)(2,1)S(1)}, bf16[128,256]{1,0:T(8,128)(2,1)S(1)}, u32[]{:S(2)}, u32[]{:S(2)}) collective-permute-start(bf16[128,256]{1,0:T(8,128)(2,1)S(1)} %get-tuple-element.23), channel_id=1, source_target_pairs={{0,2},{1,3},{2,4},{3,5},{4,6},{5,7},{6,0},{7,1},{8,10},{9,11},{10,... | collective-permute-start | bytes 196616 | tf_op jit(solution)/shard_map/ppermute | solution.py:30
  34.2 4.2 %collective-permute-done.5 = bf16[256,256]{1,0:T(8,128)(2,1)S(1)} collective-permute-done((bf16[256,256]{1,0:T(8,128)(2,1)S(1)}, bf16[256,256]{1,0:T(8,128)(2,1)S(1)}, u32[]{:S(2)}, u32[]{:S(2)}) %collective-permute-start.5) | collective-permute-done | bytes 131104 | tf_op jit(solution)/shard_map/ppermute | solution.py:30
  40.8 5.7 %collective-permute-done.7 = bf16[256,256]{1,0:T(8,128)(2,1)S(1)} collective-permute-done((bf16[256,256]{1,0:T(8,128)(2,1)S(1)}, bf16[256,256]{1,0:T(8,128)(2,1)S(1)}, u32[]{:S(2)}, u32[]{:S(2)}) %collective-permute-start.7) | collective-permute-done | bytes 131104 | tf_op jit(solution)/shard_map/ppermute | solution.py:30
  48.3 1.9 %collective-permute-start.9 = (bf16[256,256]{1,0:T(8,128)(2,1)S(1)}, bf16[256,256]{1,0:T(8,128)(2,1)S(1)}, u32[]{:S(2)}, u32[]{:S(2)}) collective-permute-start(bf16[256,256]{1,0:T(8,128)(2,1)S(1)} %add_convert_fusion.refs_0_), channel_id=1, source_target_pairs={{0,6},{1,7},{2,0},{3,1},{4,2},{5,3},{6,4},{7,5},{8,14},{9,15},{10,... | collective-permute-start | bytes 393224 | tf_op jit(solution)/shard_map/ppermute | solution.py:30
  53.9 2.9 %collective-permute-start.10 = (bf16[256,256]{1,0:T(8,128)(2,1)S(1)}, bf16[256,256]{1,0:T(8,128)(2,1)S(1)}, u32[]{:S(2)}, u32[]{:S(2)}) collective-permute-start(bf16[256,256]{1,0:T(8,128)(2,1)S(1)} %collective-permute-done.9.refs_2_), channel_id=1, source_target_pairs={{0,7},{1,0},{2,1},{3,2},{4,3},{5,4},{6,5},{7,6},{8,15},{9,8},{10,9... | collective-permute-start | bytes 393224 | tf_op jit(solution)/shard_map/ppermute | solution.py:30
  58.0 2.5 %collective-permute-start.13 = (bf16[128,256]{1,0:T(8,128)(2,1)S(1)}, bf16[128,256]{1,0:T(8,128)(2,1)S(1)}, u32[]{:S(2)}, u32[]{:S(2)}) collective-permute-start(bf16[128,256]{1,0:T(8,128)(2,1)S(1)} %slice.13), channel_id=1, source_target_pairs={{0,6},{1,7},{2,0},{3,1},{4,2},{5,3},{6,4},{7,5},{8,14},{9,15},{10,... | collective-permute-start | bytes 196616 | tf_op jit(solution)/shard_map/ppermute | solution.py:30
  62.4 2.6 %collective-permute-done.13.refs_5_ = bf16[128,256]{1,0:T(8,128)(2,1)S(1)} collective-permute-done((bf16[128,256]{1,0:T(8,128)(2,1)S(1)}, bf16[128,256]{1,0:T(8,128)(2,1)S(1)}, u32[]{:S(2)}, u32[]{:S(2)}) %collective-permute-start.13) | collective-permute-done | bytes 65568 | tf_op jit(solution)/shard_map/ppermute | solution.py:30
  65.0 3.4 %copy-done.1 = bf16[2048,2048]{1,0:T(8,128)(2,1)S(1)} copy-done((bf16[2048,2048]{1,0:T(8,128)(2,1)S(1)}, bf16[2048,2048]{1,0:T(8,128)(2,1)}, u32[]{:S(2)}) %copy-start.1) | copy-done | bytes 8388632
  68.4 3.7 %products.1 = (bf16[128,2176]{1,0:T(8,128)(2,1)S(1)}, bf16[128,2176]{1,0:T(8,128)(2,1)S(1)}, f32[96,256]{1,0:T(8,128)S(1)}, f32[96,256]{1,0:T(8,128)S(1)}, bf16[2048,256]{1,0:T(8,128)(2,1)S(1)}) custom-call(s32[4]{0:T(128)S(1)} %compare_select_fusion.2.meta, bf16[2048,2048]{1,0:T(8,128)(2,1)S(1)} %copy-done.1, bf16[16,2048]{1,0:T(8,128)(2,1)S(1)} %copy-done.5, ...), custom_call_target="tpu_custom_call" | custom-call | tf_op jit(solution)/shard_map/products/pallas_call | solution.py:183
  72.1 6.5 %collective-permute-start.24 = (bf16[128,2176]{1,0:T(8,128)(2,1)S(1)}, bf16[128,2176]{1,0:T(8,128)(2,1)S(1)}, u32[]{:S(2)}, u32[]{:S(2)}) collective-permute-start(bf16[128,2176]{1,0:T(8,128)(2,1)S(1)} %get-tuple-element.31), channel_id=1, source_target_pairs={{0,8},{8,0},{16,24},{24,16},{32,40},{40,32},{48,56},{56,48},{64,72... | collective-permute-start | bytes 1671176 | tf_op jit(solution)/shard_map/ppermute | solution.py:34
  80.3 19.9 %all_to_all.20.pieces_ref = bf16[16,8,2176]{2,1,0:T(8,128)(2,1)S(1)} all-to-all(bf16[16,8,2176]{2,1,0:T(8,128)(2,1)S(1)} %add_pair.1), channel_id=1, replica_groups={{0,16,32,48,64,80,96,112,128,144,160,176,192,208,224,240},{8,24,40,56,7..., dimensions={0} | all-to-all | bytes 1114112 | tf_op jit(solution)/shard_map/all_to_all | solution.py:397
  100.2 11.1 %all_to_all.21.slabs_ref = bf16[8,8,128]{2,1,0:T(8,128)(2,1)S(1)} all-to-all(bf16[8,8,128]{2,1,0:T(8,128)(2,1)S(1)} %get-tuple-element.33), channel_id=1, replica_groups=mesh['space'=32,'slot'=8] {'slot'}, dimensions={0} | all-to-all | bytes 32768 | tf_op jit(solution)/shard_map/all_to_all | solution.py:397
  112.7 3.6 %all-to-all-start.3 = ((bf16[16,8,2048]{2,1,0:T(8,128)(2,1)}), bf16[16,8,2048]{2,1,0:T(8,128)(2,1)S(1)}, u32[]{:S(2)}, u32[]{:S(2)}) async-start(bf16[16,8,2048]{2,1,0:T(8,128)(2,1)} %insert.1), calls=%async_computation.3 | async-start | bytes 1048576 | tf_op jit(solution)/shard_map/all_to_all | solution.py:397
  116.3 3.3 %collective-permute-start.16 = (f32[96,256]{1,0:T(8,128)S(1)}, f32[96,256]{1,0:T(8,128)S(1)}, u32[]{:S(2)}, u32[]{:S(2)}) collective-permute-start(f32[96,256]{1,0:T(8,128)S(1)} %get-tuple-element.28), channel_id=1, source_target_pairs={{0,8},{8,0},{16,24},{24,16},{32,40},{40,32},{48,56},{56,48},{64,72... | collective-permute-start | bytes 294920 | tf_op jit(solution)/shard_map/ppermute | solution.py:34
  120.6 2.7 %collective-permute-start.19 = (f32[96,256]{1,0:T(8,128)S(1)}, f32[96,256]{1,0:T(8,128)S(1)}, u32[]{:S(2)}, u32[]{:S(2)}) collective-permute-start(f32[96,256]{1,0:T(8,128)S(1)} %add.61), channel_id=1, source_target_pairs={{0,48},{8,56},{16,0},{24,8},{32,16},{40,24},{48,32},{56,40},{64,11... | collective-permute-start | bytes 294920 | tf_op jit(solution)/shard_map/ppermute | solution.py:34
  125.2 5.1 %collective-permute-start.25 = (bf16[128,2048]{1,0:T(8,128)(2,1)S(1)}, bf16[128,2048]{1,0:T(8,128)(2,1)S(1)}, u32[]{:S(2)}, u32[]{:S(2)}) collective-permute-start(bf16[128,2048]{1,0:T(8,128)(2,1)S(1)} %bitcast.11), channel_id=1, source_target_pairs={{0,8},{8,0},{16,24},{24,16},{32,40},{40,32},{48,56},{56,48},{64,72... | collective-permute-start | bytes 1572872 | tf_op jit(solution)/shard_map/ppermute | solution.py:34
  130.5 2.6 %collective-permute-start.22 = (f32[96,256]{1,0:T(8,128)S(1)}, f32[96,256]{1,0:T(8,128)S(1)}, u32[]{:S(2)}, u32[]{:S(2)}) collective-permute-start(f32[96,256]{1,0:T(8,128)S(1)} %add_add_fusion.1), channel_id=1, source_target_pairs={{0,192},{8,200},{16,208},{24,216},{32,224},{40,232},{48,240},{56,2... | collective-permute-start | bytes 294920 | tf_op jit(solution)/shard_map/ppermute | solution.py:34
  134.8 4.0 %collective-permute-done.21 = f32[96,256]{1,0:T(8,128)S(1)} collective-permute-done((f32[96,256]{1,0:T(8,128)S(1)}, f32[96,256]{1,0:T(8,128)S(1)}, u32[]{:S(2)}, u32[]{:S(2)}) %collective-permute-start.21) | collective-permute-done | bytes 98336 | tf_op jit(solution)/shard_map/ppermute | solution.py:34
  138.9 3.1 %collective-permute-start.23 = (f32[96,256]{1,0:T(8,128)S(1)}, f32[96,256]{1,0:T(8,128)S(1)}, u32[]{:S(2)}, u32[]{:S(2)}) collective-permute-start(f32[96,256]{1,0:T(8,128)S(1)} %add_add_fusion.mine_ref), channel_id=1, source_target_pairs={{0,8},{8,0},{16,24},{24,16},{32,40},{40,32},{48,56},{56,48},{64,72... | collective-permute-start | bytes 294920 | tf_op jit(solution)/shard_map/ppermute | solution.py:34
  142.9 9.5 %invert.1.inverse_ref = f32[256,256]{1,0:T(8,128)S(1)} custom-call(s32[4]{0:T(128)S(1)} %compare_select_fusion.2.meta, f32[96,256]{1,0:T(8,128)S(1)} %add_add_fusion.mine_ref, f32[96,256]{1,0:T(8,128)S(1)} %collective-permute-done.23.other_ref), custom_call_target="tpu_custom_call" | custom-call | tf_op jit(solution)/shard_map/invert/pallas_call | solution.py:346
  154.1 2.6 %coefs.1 = f32[256,2048]{1,0:T(8,128)} custom-call(s32[4]{0:T(128)S(1)} %compare_select_fusion.2.meta, f32[256,256]{1,0:T(8,128)S(1)} %invert.1.inverse_ref, bf16[128,2048]{1,0:T(8,128)(2,1)S(1)} %bitcast.12, bf16[128,2048]{1,0:T(8,128)(2,1)S(1)} %collective-permute-done.25.other_ref), custom_call_target="tpu_custom_call" | custom-call | tf_op jit(solution)/shard_map/coefs/pallas_call | solution.py:385
  (66 shorter events, 36.5 us)
Async XLA Ops:
  3.0 19.5 %all-to-all-start = ((bf16[8,64,256]{2,1,0:T(8,128)(2,1)}), bf16[8,64,256]{2,1,0:T(8,128)(2,1)S(1)}, u32[]{:S(2)}, u32[]{:S(2)}) async-start(bf16[8,64,256]{2,1,0:T(8,128)(2,1)} %bitcast.4), calls=%async_computation | async-start | bytes 524288 | tf_op jit(solution)/shard_map/all_to_all | solution.py:422
  23.9 9.0 %collective-permute-start.2 = (bf16[256,256]{1,0:T(8,128)(2,1)S(1)}, bf16[256,256]{1,0:T(8,128)(2,1)S(1)}, u32[]{:S(2)}, u32[]{:S(2)}) collective-permute-start(bf16[256,256]{1,0:T(8,128)(2,1)S(1)} %get-tuple-element.22), channel_id=1, source_target_pairs={{0,1},{1,2},{2,3},{3,4},{4,5},{5,6},{6,7},{7,0},{8,9},{9,10},{10,1... | collective-permute-start | bytes 393224 | tf_op jit(solution)/shard_map/ppermute | solution.py:30
  25.4 6.4 %collective-permute-start.3 = (bf16[128,256]{1,0:T(8,128)(2,1)S(1)}, bf16[128,256]{1,0:T(8,128)(2,1)S(1)}, u32[]{:S(2)}, u32[]{:S(2)}) collective-permute-start(bf16[128,256]{1,0:T(8,128)(2,1)S(1)} %get-tuple-element.23), channel_id=1, source_target_pairs={{0,2},{1,3},{2,4},{3,5},{4,6},{5,7},{6,0},{7,1},{8,10},{9,11},{10,... | collective-permute-start | bytes 196616 | tf_op jit(solution)/shard_map/ppermute | solution.py:30
  27.5 6.7 %collective-permute-start.6 = (bf16[128,256]{1,0:T(8,128)(2,1)S(1)}, bf16[128,256]{1,0:T(8,128)(2,1)S(1)}, u32[]{:S(2)}, u32[]{:S(2)}) collective-permute-start(bf16[128,256]{1,0:T(8,128)(2,1)S(1)} %get-tuple-element.26), channel_id=1, source_target_pairs={{0,6},{1,7},{2,0},{3,1},{4,2},{5,3},{6,4},{7,5},{8,14},{9,15},{10,... | collective-permute-start | bytes 196616 | tf_op jit(solution)/shard_map/ppermute | solution.py:30
  29.0 11.0 %collective-permute-start = (bf16[256,256]{1,0:T(8,128)(2,1)S(1)}, bf16[256,256]{1,0:T(8,128)(2,1)S(1)}, u32[]{:S(2)}, u32[]{:S(2)}) collective-permute-start(bf16[256,256]{1,0:T(8,128)(2,1)S(1)} %get-tuple-element.19), channel_id=1, source_target_pairs={{0,1},{1,2},{2,3},{3,4},{4,5},{5,6},{6,7},{7,0},{8,9},{9,10},{10,1... | collective-permute-start | bytes 393224 | tf_op jit(solution)/shard_map/ppermute | solution.py:30
  30.2 9.8 %collective-permute-start.1 = (bf16[256,256]{1,0:T(8,128)(2,1)S(1)}, bf16[256,256]{1,0:T(8,128)(2,1)S(1)}, u32[]{:S(2)}, u32[]{:S(2)}) collective-permute-start(bf16[256,256]{1,0:T(8,128)(2,1)S(1)} %get-tuple-element.20), channel_id=1, source_target_pairs={{0,7},{1,0},{2,1},{3,2},{4,3},{5,4},{6,5},{7,6},{8,15},{9,8},{10,9... | collective-permute-start | bytes 393224 | tf_op jit(solution)/shard_map/ppermute | solution.py:30
  31.8 6.7 %collective-permute-start.5 = (bf16[256,256]{1,0:T(8,128)(2,1)S(1)}, bf16[256,256]{1,0:T(8,128)(2,1)S(1)}, u32[]{:S(2)}, u32[]{:S(2)}) collective-permute-start(bf16[256,256]{1,0:T(8,128)(2,1)S(1)} %get-tuple-element.25), channel_id=1, source_target_pairs={{0,7},{1,0},{2,1},{3,2},{4,3},{5,4},{6,5},{7,6},{8,15},{9,8},{10,9... | collective-permute-start | bytes 393224 | tf_op jit(solution)/shard_map/ppermute | solution.py:30
  33.0 7.8 %collective-permute-start.4 = (bf16[256,256]{1,0:T(8,128)(2,1)S(1)}, bf16[256,256]{1,0:T(8,128)(2,1)S(1)}, u32[]{:S(2)}, u32[]{:S(2)}) collective-permute-start(bf16[256,256]{1,0:T(8,128)(2,1)S(1)} %add_convert_fusion.2), channel_id=1, source_target_pairs={{0,2},{1,3},{2,4},{3,5},{4,6},{5,7},{6,0},{7,1},{8,10},{9,11},{10,... | collective-permute-start | bytes 393224 | tf_op jit(solution)/shard_map/ppermute | solution.py:30
  38.5 8.0 %collective-permute-start.7 = (bf16[256,256]{1,0:T(8,128)(2,1)S(1)}, bf16[256,256]{1,0:T(8,128)(2,1)S(1)}, u32[]{:S(2)}, u32[]{:S(2)}) collective-permute-start(bf16[256,256]{1,0:T(8,128)(2,1)S(1)} %add_convert_fusion.1), channel_id=1, source_target_pairs={{0,6},{1,7},{2,0},{3,1},{4,2},{5,3},{6,4},{7,5},{8,14},{9,15},{10,... | collective-permute-start | bytes 393224 | tf_op jit(solution)/shard_map/ppermute | solution.py:30
  46.6 7.3 %collective-permute-start.11 = (bf16[256,256]{1,0:T(8,128)(2,1)S(1)}, bf16[256,256]{1,0:T(8,128)(2,1)S(1)}, u32[]{:S(2)}, u32[]{:S(2)}) collective-permute-start(bf16[256,256]{1,0:T(8,128)(2,1)S(1)} %add_convert_fusion.refs_0_), channel_id=1, source_target_pairs={{0,2},{1,3},{2,4},{3,5},{4,6},{5,7},{6,0},{7,1},{8,10},{9,11},{10,... | collective-permute-start | bytes 393224 | tf_op jit(solution)/shard_map/ppermute | solution.py:30
  48.3 5.6 %collective-permute-start.9 = (bf16[256,256]{1,0:T(8,128)(2,1)S(1)}, bf16[256,256]{1,0:T(8,128)(2,1)S(1)}, u32[]{:S(2)}, u32[]{:S(2)}) collective-permute-start(bf16[256,256]{1,0:T(8,128)(2,1)S(1)} %add_convert_fusion.refs_0_), channel_id=1, source_target_pairs={{0,6},{1,7},{2,0},{3,1},{4,2},{5,3},{6,4},{7,5},{8,14},{9,15},{10,... | collective-permute-start | bytes 393224 | tf_op jit(solution)/shard_map/ppermute | solution.py:30
  50.2 7.8 %collective-permute-start.15 = (bf16[256,256]{1,0:T(8,128)(2,1)S(1)}, bf16[256,256]{1,0:T(8,128)(2,1)S(1)}, u32[]{:S(2)}, u32[]{:S(2)}) collective-permute-start(bf16[256,256]{1,0:T(8,128)(2,1)S(1)} %add_convert_fusion.refs_0_), channel_id=1, source_target_pairs={{0,1},{1,2},{2,3},{3,4},{4,5},{5,6},{6,7},{7,0},{8,9},{9,10},{10,1... | collective-permute-start | bytes 393224 | tf_op jit(solution)/shard_map/ppermute | solution.py:30
  51.6 8.9 %collective-permute-start.8 = (bf16[256,256]{1,0:T(8,128)(2,1)S(1)}, bf16[256,256]{1,0:T(8,128)(2,1)S(1)}, u32[]{:S(2)}, u32[]{:S(2)}) collective-permute-start(bf16[256,256]{1,0:T(8,128)(2,1)S(1)} %add_convert_fusion.refs_0_), channel_id=1, source_target_pairs={{0,7},{1,0},{2,1},{3,2},{4,3},{5,4},{6,5},{7,6},{8,15},{9,8},{10,9... | collective-permute-start | bytes 393224 | tf_op jit(solution)/shard_map/ppermute | solution.py:30
  53.9 11.0 %collective-permute-start.14 = (bf16[256,256]{1,0:T(8,128)(2,1)S(1)}, bf16[256,256]{1,0:T(8,128)(2,1)S(1)}, u32[]{:S(2)}, u32[]{:S(2)}) collective-permute-start(bf16[256,256]{1,0:T(8,128)(2,1)S(1)} %collective-permute-done.11.refs_7_), channel_id=1, source_target_pairs={{0,1},{1,2},{2,3},{3,4},{4,5},{5,6},{6,7},{7,0},{8,9},{9,10},{10,1... | collective-permute-start | bytes 393224 | tf_op jit(solution)/shard_map/ppermute | solution.py:30
  53.9 11.0 %collective-permute-start.10 = (bf16[256,256]{1,0:T(8,128)(2,1)S(1)}, bf16[256,256]{1,0:T(8,128)(2,1)S(1)}, u32[]{:S(2)}, u32[]{:S(2)}) collective-permute-start(bf16[256,256]{1,0:T(8,128)(2,1)S(1)} %collective-permute-done.9.refs_2_), channel_id=1, source_target_pairs={{0,7},{1,0},{2,1},{3,2},{4,3},{5,4},{6,5},{7,6},{8,15},{9,8},{10,9... | collective-permute-start | bytes 393224 | tf_op jit(solution)/shard_map/ppermute | solution.py:30
  58.0 6.9 %collective-permute-start.13 = (bf16[128,256]{1,0:T(8,128)(2,1)S(1)}, bf16[128,256]{1,0:T(8,128)(2,1)S(1)}, u32[]{:S(2)}, u32[]{:S(2)}) collective-permute-start(bf16[128,256]{1,0:T(8,128)(2,1)S(1)} %slice.13), channel_id=1, source_target_pairs={{0,6},{1,7},{2,0},{3,1},{4,2},{5,3},{6,4},{7,5},{8,14},{9,15},{10,... | collective-permute-start | bytes 196616 | tf_op jit(solution)/shard_map/ppermute | solution.py:30
  72.1 8.1 %collective-permute-start.24 = (bf16[128,2176]{1,0:T(8,128)(2,1)S(1)}, bf16[128,2176]{1,0:T(8,128)(2,1)S(1)}, u32[]{:S(2)}, u32[]{:S(2)}) collective-permute-start(bf16[128,2176]{1,0:T(8,128)(2,1)S(1)} %get-tuple-element.31), channel_id=1, source_target_pairs={{0,8},{8,0},{16,24},{24,16},{32,40},{40,32},{48,56},{56,48},{64,72... | collective-permute-start | bytes 1671176 | tf_op jit(solution)/shard_map/ppermute | solution.py:34
  112.7 12.5 %all-to-all-start.3 = ((bf16[16,8,2048]{2,1,0:T(8,128)(2,1)}), bf16[16,8,2048]{2,1,0:T(8,128)(2,1)S(1)}, u32[]{:S(2)}, u32[]{:S(2)}) async-start(bf16[16,8,2048]{2,1,0:T(8,128)(2,1)} %insert.1), calls=%async_computation.3 | async-start | bytes 1048576 | tf_op jit(solution)/shard_map/all_to_all | solution.py:397
  120.6 9.8 %collective-permute-start.19 = (f32[96,256]{1,0:T(8,128)S(1)}, f32[96,256]{1,0:T(8,128)S(1)}, u32[]{:S(2)}, u32[]{:S(2)}) collective-permute-start(f32[96,256]{1,0:T(8,128)S(1)} %add.61), channel_id=1, source_target_pairs={{0,48},{8,56},{16,0},{24,8},{32,16},{40,24},{48,32},{56,40},{64,11... | collective-permute-start | bytes 294920 | tf_op jit(solution)/shard_map/ppermute | solution.py:34
  123.3 7.1 %collective-permute-start.18 = (f32[96,256]{1,0:T(8,128)S(1)}, f32[96,256]{1,0:T(8,128)S(1)}, u32[]{:S(2)}, u32[]{:S(2)}) collective-permute-start(f32[96,256]{1,0:T(8,128)S(1)} %add.61), channel_id=1, source_target_pairs={{0,16},{8,24},{16,32},{24,40},{32,48},{40,56},{48,0},{56,8},{64,80... | collective-permute-start | bytes 294920 | tf_op jit(solution)/shard_map/ppermute | solution.py:34
  123.3 7.2 %collective-permute-start.17 = (f32[96,256]{1,0:T(8,128)S(1)}, f32[96,256]{1,0:T(8,128)S(1)}, u32[]{:S(2)}, u32[]{:S(2)}) collective-permute-start(f32[96,256]{1,0:T(8,128)S(1)} %add.61), channel_id=1, source_target_pairs={{0,32},{8,40},{16,48},{24,56},{32,0},{40,8},{48,16},{56,24},{64,96... | collective-permute-start | bytes 294920 | tf_op jit(solution)/shard_map/ppermute | solution.py:34
  125.2 28.9 %collective-permute-start.25 = (bf16[128,2048]{1,0:T(8,128)(2,1)S(1)}, bf16[128,2048]{1,0:T(8,128)(2,1)S(1)}, u32[]{:S(2)}, u32[]{:S(2)}) collective-permute-start(bf16[128,2048]{1,0:T(8,128)(2,1)S(1)} %bitcast.11), channel_id=1, source_target_pairs={{0,8},{8,0},{16,24},{24,16},{32,40},{40,32},{48,56},{56,48},{64,72... | collective-permute-start | bytes 1572872 | tf_op jit(solution)/shard_map/ppermute | solution.py:34
  133.1 5.7 %collective-permute-start.21 = (f32[96,256]{1,0:T(8,128)S(1)}, f32[96,256]{1,0:T(8,128)S(1)}, u32[]{:S(2)}, u32[]{:S(2)}) collective-permute-start(f32[96,256]{1,0:T(8,128)S(1)} %add_add_fusion.1), channel_id=1, source_target_pairs={{0,64},{8,72},{16,80},{24,88},{32,96},{40,104},{48,112},{56,120},{... | collective-permute-start | bytes 294920 | tf_op jit(solution)/shard_map/ppermute | solution.py:34
  133.1 5.7 %collective-permute-start.20 = (f32[96,256]{1,0:T(8,128)S(1)}, f32[96,256]{1,0:T(8,128)S(1)}, u32[]{:S(2)}, u32[]{:S(2)}) collective-permute-start(f32[96,256]{1,0:T(8,128)S(1)} %add_add_fusion.1), channel_id=1, source_target_pairs={{0,128},{8,136},{16,144},{24,152},{32,160},{40,168},{48,176},{56,1... | collective-permute-start | bytes 294920 | tf_op jit(solution)/shard_map/ppermute | solution.py:34
  (10 other events, 72.4 us)
where the time goes:
time: 157 us
  starting transfers between devices  63.9 us (41%)
  blocking collectives  30.9 us (20%)
  waiting for transfers between devices  24.2 us (15%)
  Pallas kernels  23.4 us (15%)
  local copies, waits for them, and re-layouts  11.3 us (7%)
  between operations  2.07 us (1%)
    all_to_all x2, blocking collectives, exchange(): lax.all_to_all(value, axis, 0, 0, axis_index_groups=groups, tiled=True)  30.9 us
    ppermute x10, starting transfers between devices, along(): return lax.ppermute(value, 'space', space_shift(dy, dx, dc))  26.8 us
    ppermute x16, starting transfers between devices, ring(): lax.ppermute(value, 'slot', [(i, (i + distance) % size) for i in range(si...  24.5 us
    ppermute x16, waiting for transfers between devices, ring(): lax.ppermute(value, 'slot', [(i, (i + distance) % size) for i in range(si...  16.3 us
    unnamed x13, local copies, waits for them, and re-layouts  9.6 us
    pallas_call x1, Pallas kernels, invert(): pl.pallas_call(functools.partial(factor_kernel, row_total), in_specs=[SME...  9.5 us
    all_to_all x1, starting transfers between devices, local(): lax.all_to_all(test_rows.reshape(slots, width, rank), 'slot', 0, 0, tiled...  9 us
    ppermute x10, waiting for transfers between devices, along(): return lax.ppermute(value, 'space', space_shift(dy, dx, dc))  7.63 us
  transfers between devices with their start and end apart: 28, of which 14 were waited for; matrix products, arithmetic and copies ran while one was open for 1% of the time, Pallas kernels for 9%

commit v1 on v0

--- a/solution.py
+++ b/solution.py
@@ -14,6 +14,7 @@
 HIGHEST = lax.Precision.HIGHEST
 
 CORES = 2
+CHUNKS = 4
 
 
 def space_shift(dy, dx, dc=0):
@@ -139,9 +140,18 @@
 
 
 def cross_kernel(parts, meta, values_ref, scales_ref, slab_ref, slab_scales_ref, *refs):
-    sketch_refs, refs = refs[:-9], refs[-9:]
+    sketch_refs, refs = refs[:-11], refs[-11:]
     mine_ref, theirs_ref, gram_mine_ref, gram_theirs_ref, sketch_ref = refs[:5]
-    cross_ref, gram_ref, scale_ref, slab_scale_ref = refs[5:]
+    cross_ref, gram_ref, scale_ref, slab_scale_ref = refs[5:9]
+    window_ref, arrived = refs[9:]
+    chunk = values_ref.shape[0] // CHUNKS
+    copies = []
+    for i in range(CHUNKS):
+        lines = pl.ds(chunk * i, chunk)
+        copies.append(
+            pltpu.make_async_copy(values_ref.at[lines, :], window_ref.at[lines, :], arrived.at[i])
+        )
+        copies[-1].start()
     gather_blocks(parts, meta, sketch_refs, sketch_ref)
     scale_ref[...] = scales_ref[...].astype(F32)
     slab_scale_ref[...] = slab_scales_ref[...].astype(F32)
@@ -160,9 +170,10 @@
     slab = expand_slab(slab_ref, slab_scale_ref, row_blocks)
     cross_ref[:, cols:] = jnp.zeros((rank, cross_ref.shape[1] - cols), F32)
     cross_ref[:, cols : cols + width] = contract(sketch, slab, 0, 1)
-    count = row_blocks // 2
+    count = row_blocks // CHUNKS
     for first in range(0, row_blocks, count):
-        window = expand(values_ref, scale_ref, first, count)
+        copies[first // count].wait()
+        window = expand(window_ref, scale_ref, first, count)
         part = contract(sketch[BLOCK * first : BLOCK * (first + count), :], window, 0, 0)
         cross_ref[:, :cols] = part if first == 0 else cross_ref[:, :cols] + part
     core = meta[1]
@@ -182,7 +193,7 @@
     gram_half = (3 * rank // 8, rank)
     return pl.pallas_call(
         functools.partial(cross_kernel, parts),
-        in_specs=[SMEM] + [VMEM] * (4 + len(sketch_blocks)),
+        in_specs=[SMEM, pl.BlockSpec(memory_space=pltpu.HBM)] + [VMEM] * (3 + len(sketch_blocks)),
         out_specs=[VMEM] * 5,
         out_shape=[jax.ShapeDtypeStruct((half, lanes), BF16)] * 2
         + [jax.ShapeDtypeStruct(gram_half, F32)] * 2
@@ -192,6 +203,8 @@
             pltpu.VMEM((CORES, *gram_half), F32),
             pltpu.VMEM(scales.shape, F32),
             pltpu.VMEM(slab_scales.shape, F32),
+            pltpu.VMEM(values.shape, BF16),
+            pltpu.SemaphoreType.DMA((CHUNKS,)),
         ],
         compiler_params=pltpu.CompilerParams(vmem_limit_bytes=40 * 2**20),
         name="products",
@@ -420,8 +433,8 @@
 
     test_rows = lax.dynamic_slice_in_dim(test_matrix, first, SLAB, 0)
     tests = lax.all_to_all(test_rows.reshape(slots, width, rank), "slot", 0, 0, tiled=True)
-    window_values = pltpu.with_memory_space_constraint(window_values, pltpu.VMEM)
-    partial = sketch_window(meta, window_values, window_scales, test_matrix)
+    resident = pltpu.with_memory_space_constraint(window_values, pltpu.VMEM)
+    partial = sketch_window(meta, resident, window_scales, test_matrix)
     slab, slab_scale = slab_values.T, slab_scales.T
     x0, x1, x2, x3, x4a, x4b, x5, x6, x7 = add_slab(
         meta, partial, slab, slab_scale, tests, slots

time: 157 us -> 158 us (level)
  no operation moved by 1% of the time
where the time goes in v1:
time: 158 us
  starting transfers between devices  63.9 us (40%)
  blocking collectives  30.9 us (20%)
  Pallas kernels  24.4 us (15%)
  waiting for transfers between devices  24.2 us (15%)
  local copies, waits for them, and re-layouts  11.3 us (7%)
  between operations  2.07 us (1%)
    all_to_all x2, blocking collectives, exchange(): lax.all_to_all(value, axis, 0, 0, axis_index_groups=groups, tiled=True)  30.9 us
    ppermute x10, starting transfers between devices, along(): return lax.ppermute(value, 'space', space_shift(dy, dx, dc))  26.8 us
    ppermute x16, starting transfers between devices, ring(): lax.ppermute(value, 'slot', [(i, (i + distance) % size) for i in range(si...  24.5 us
    ppermute x16, waiting for transfers between devices, ring(): lax.ppermute(value, 'slot', [(i, (i + distance) % size) for i in range(si...  16.3 us
    unnamed x13, local copies, waits for them, and re-layouts  9.6 us
    pallas_call x1, Pallas kernels, invert(): pl.pallas_call(functools.partial(factor_kernel, row_total), in_specs=[SME...  9.5 us
    all_to_all x1, starting transfers between devices, local(): lax.all_to_all(test_rows.reshape(slots, width, rank), 'slot', 0, 0, tiled...  9 us
    ppermute x10, waiting for transfers between devices, along(): return lax.ppermute(value, 'space', space_shift(dy, dx, dc))  7.63 us
  transfers between devices with their start and end apart: 28, of which 14 were waited for; matrix products, arithmetic and copies ran while one was open for 1% of the time, Pallas kernels for 9%

profile of v1, /device:TPU:1, one launch (start us, length us, event | category | flops | bytes accessed | tf_op | source)
XLA Modules:
  0.0 157.8 jit_solution(3636248479627159403)
XLA Ops:
  3.0 9.0 %all-to-all-start = ((bf16[8,64,256]{2,1,0:T(8,128)(2,1)}), bf16[8,64,256]{2,1,0:T(8,128)(2,1)S(1)}, u32[]{:S(2)}, u32[]{:S(2)}) async-start(bf16[8,64,256]{2,1,0:T(8,128)(2,1)} %bitcast.4), calls=%async_computation | async-start | bytes 524288 | tf_op jit(solution)/shard_map/all_to_all | solution.py:435
  14.1 3.4 %copy-done = bf16[2048,2048]{1,0:T(8,128)(2,1)S(1)} copy-done((bf16[2048,2048]{1,0:T(8,128)(2,1)S(1)}, bf16[2048,2048]{1,0:T(8,128)(2,1)}, u32[]{:S(2)}) %copy-start) | copy-done | bytes 8388632
  19.6 2.9 %sketch_window.1.partial_ref = f32[2048,256]{1,0:T(8,128)S(1)} custom-call(s32[4]{0:T(128)S(1)} %compare_select_fusion.2.meta, bf16[2048,2048]{1,0:T(8,128)(2,1)S(1)} %copy-done, bf16[16,2048]{1,0:T(8,128)(2,1)S(1)} %copy-done.4, bf16[2048,256]{1,0:T(8,128)(2,1)S(1)} %copy-done.2), custom_call_target="tpu_custom_call" | custom-call | tf_op jit(solution)/shard_map/sketch_window/pallas_call | solution.py:91
  25.4 2.1 %collective-permute-start.3 = (bf16[128,256]{1,0:T(8,128)(2,1)S(1)}, bf16[128,256]{1,0:T(8,128)(2,1)S(1)}, u32[]{:S(2)}, u32[]{:S(2)}) collective-permute-start(bf16[128,256]{1,0:T(8,128)(2,1)S(1)} %get-tuple-element.23), channel_id=1, source_target_pairs={{0,2},{1,3},{2,4},{3,5},{4,6},{5,7},{6,0},{7,1},{8,10},{9,11},{10,... | collective-permute-start | bytes 196616 | tf_op jit(solution)/shard_map/ppermute | solution.py:31
  34.2 4.2 %collective-permute-done.5 = bf16[256,256]{1,0:T(8,128)(2,1)S(1)} collective-permute-done((bf16[256,256]{1,0:T(8,128)(2,1)S(1)}, bf16[256,256]{1,0:T(8,128)(2,1)S(1)}, u32[]{:S(2)}, u32[]{:S(2)}) %collective-permute-start.5) | collective-permute-done | bytes 131104 | tf_op jit(solution)/shard_map/ppermute | solution.py:31
  40.8 5.7 %collective-permute-done.7 = bf16[256,256]{1,0:T(8,128)(2,1)S(1)} collective-permute-done((bf16[256,256]{1,0:T(8,128)(2,1)S(1)}, bf16[256,256]{1,0:T(8,128)(2,1)S(1)}, u32[]{:S(2)}, u32[]{:S(2)}) %collective-permute-start.7) | collective-permute-done | bytes 131104 | tf_op jit(solution)/shard_map/ppermute | solution.py:31
  48.3 1.9 %collective-permute-start.9 = (bf16[256,256]{1,0:T(8,128)(2,1)S(1)}, bf16[256,256]{1,0:T(8,128)(2,1)S(1)}, u32[]{:S(2)}, u32[]{:S(2)}) collective-permute-start(bf16[256,256]{1,0:T(8,128)(2,1)S(1)} %add_convert_fusion.refs_0_), channel_id=1, source_target_pairs={{0,6},{1,7},{2,0},{3,1},{4,2},{5,3},{6,4},{7,5},{8,14},{9,15},{10,... | collective-permute-start | bytes 393224 | tf_op jit(solution)/shard_map/ppermute | solution.py:31
  53.9 2.9 %collective-permute-start.10 = (bf16[256,256]{1,0:T(8,128)(2,1)S(1)}, bf16[256,256]{1,0:T(8,128)(2,1)S(1)}, u32[]{:S(2)}, u32[]{:S(2)}) collective-permute-start(bf16[256,256]{1,0:T(8,128)(2,1)S(1)} %collective-permute-done.9.refs_2_), channel_id=1, source_target_pairs={{0,7},{1,0},{2,1},{3,2},{4,3},{5,4},{6,5},{7,6},{8,15},{9,8},{10,9... | collective-permute-start | bytes 393224 | tf_op jit(solution)/shard_map/ppermute | solution.py:31
  58.0 2.5 %collective-permute-start.13 = (bf16[128,256]{1,0:T(8,128)(2,1)S(1)}, bf16[128,256]{1,0:T(8,128)(2,1)S(1)}, u32[]{:S(2)}, u32[]{:S(2)}) collective-permute-start(bf16[128,256]{1,0:T(8,128)(2,1)S(1)} %slice.13), channel_id=1, source_target_pairs={{0,6},{1,7},{2,0},{3,1},{4,2},{5,3},{6,4},{7,5},{8,14},{9,15},{10,... | collective-permute-start | bytes 196616 | tf_op jit(solution)/shard_map/ppermute | solution.py:31
  62.4 2.6 %collective-permute-done.13.refs_5_ = bf16[128,256]{1,0:T(8,128)(2,1)S(1)} collective-permute-done((bf16[128,256]{1,0:T(8,128)(2,1)S(1)}, bf16[128,256]{1,0:T(8,128)(2,1)S(1)}, u32[]{:S(2)}, u32[]{:S(2)}) %collective-permute-start.13) | collective-permute-done | bytes 65568 | tf_op jit(solution)/shard_map/ppermute | solution.py:31
  65.0 3.4 %copy-done.1 = bf16[2048,2048]{1,0:T(8,128)(2,1)S(1)} copy-done((bf16[2048,2048]{1,0:T(8,128)(2,1)S(1)}, bf16[2048,2048]{1,0:T(8,128)(2,1)}, u32[]{:S(2)}) %copy-start.1) | copy-done | bytes 8388632
  68.4 4.7 %products.1 = (bf16[128,2176]{1,0:T(8,128)(2,1)S(1)}, bf16[128,2176]{1,0:T(8,128)(2,1)S(1)}, f32[96,256]{1,0:T(8,128)S(1)}, f32[96,256]{1,0:T(8,128)S(1)}, bf16[2048,256]{1,0:T(8,128)(2,1)S(1)}) custom-call(s32[4]{0:T(128)S(1)} %compare_select_fusion.2.meta, bf16[2048,2048]{1,0:T(8,128)(2,1)S(1)} %copy-done.1, bf16[16,2048]{1,0:T(8,128)(2,1)S(1)} %copy-done.5, ...), custom_call_target="tpu_custom_call" | custom-call | tf_op jit(solution)/shard_map/products/pallas_call | solution.py:194
  73.1 6.5 %collective-permute-start.24 = (bf16[128,2176]{1,0:T(8,128)(2,1)S(1)}, bf16[128,2176]{1,0:T(8,128)(2,1)S(1)}, u32[]{:S(2)}, u32[]{:S(2)}) collective-permute-start(bf16[128,2176]{1,0:T(8,128)(2,1)S(1)} %get-tuple-element.31), channel_id=1, source_target_pairs={{0,8},{8,0},{16,24},{24,16},{32,40},{40,32},{48,56},{56,48},{64,72... | collective-permute-start | bytes 1671176 | tf_op jit(solution)/shard_map/ppermute | solution.py:35
  81.3 19.9 %all_to_all.20.pieces_ref = bf16[16,8,2176]{2,1,0:T(8,128)(2,1)S(1)} all-to-all(bf16[16,8,2176]{2,1,0:T(8,128)(2,1)S(1)} %add_pair.1), channel_id=1, replica_groups={{0,16,32,48,64,80,96,112,128,144,160,176,192,208,224,240},{8,24,40,56,7..., dimensions={0} | all-to-all | bytes 1114112 | tf_op jit(solution)/shard_map/all_to_all | solution.py:410
  101.2 11.1 %all_to_all.21.slabs_ref = bf16[8,8,128]{2,1,0:T(8,128)(2,1)S(1)} all-to-all(bf16[8,8,128]{2,1,0:T(8,128)(2,1)S(1)} %get-tuple-element.33), channel_id=1, replica_groups=mesh['space'=32,'slot'=8] {'slot'}, dimensions={0} | all-to-all | bytes 32768 | tf_op jit(solution)/shard_map/all_to_all | solution.py:410
  113.7 3.6 %all-to-all-start.3 = ((bf16[16,8,2048]{2,1,0:T(8,128)(2,1)}), bf16[16,8,2048]{2,1,0:T(8,128)(2,1)S(1)}, u32[]{:S(2)}, u32[]{:S(2)}) async-start(bf16[16,8,2048]{2,1,0:T(8,128)(2,1)} %insert.1), calls=%async_computation.3 | async-start | bytes 1048576 | tf_op jit(solution)/shard_map/all_to_all | solution.py:410
  117.3 3.3 %collective-permute-start.16 = (f32[96,256]{1,0:T(8,128)S(1)}, f32[96,256]{1,0:T(8,128)S(1)}, u32[]{:S(2)}, u32[]{:S(2)}) collective-permute-start(f32[96,256]{1,0:T(8,128)S(1)} %get-tuple-element.28), channel_id=1, source_target_pairs={{0,8},{8,0},{16,24},{24,16},{32,40},{40,32},{48,56},{56,48},{64,72... | collective-permute-start | bytes 294920 | tf_op jit(solution)/shard_map/ppermute | solution.py:35
  121.6 2.7 %collective-permute-start.19 = (f32[96,256]{1,0:T(8,128)S(1)}, f32[96,256]{1,0:T(8,128)S(1)}, u32[]{:S(2)}, u32[]{:S(2)}) collective-permute-start(f32[96,256]{1,0:T(8,128)S(1)} %add.61), channel_id=1, source_target_pairs={{0,48},{8,56},{16,0},{24,8},{32,16},{40,24},{48,32},{56,40},{64,11... | collective-permute-start | bytes 294920 | tf_op jit(solution)/shard_map/ppermute | solution.py:35
  126.3 5.1 %collective-permute-start.25 = (bf16[128,2048]{1,0:T(8,128)(2,1)S(1)}, bf16[128,2048]{1,0:T(8,128)(2,1)S(1)}, u32[]{:S(2)}, u32[]{:S(2)}) collective-permute-start(bf16[128,2048]{1,0:T(8,128)(2,1)S(1)} %bitcast.11), channel_id=1, source_target_pairs={{0,8},{8,0},{16,24},{24,16},{32,40},{40,32},{48,56},{56,48},{64,72... | collective-permute-start | bytes 1572872 | tf_op jit(solution)/shard_map/ppermute | solution.py:35
  131.6 2.6 %collective-permute-start.22 = (f32[96,256]{1,0:T(8,128)S(1)}, f32[96,256]{1,0:T(8,128)S(1)}, u32[]{:S(2)}, u32[]{:S(2)}) collective-permute-start(f32[96,256]{1,0:T(8,128)S(1)} %add_add_fusion.1), channel_id=1, source_target_pairs={{0,192},{8,200},{16,208},{24,216},{32,224},{40,232},{48,240},{56,2... | collective-permute-start | bytes 294920 | tf_op jit(solution)/shard_map/ppermute | solution.py:35
  135.9 4.0 %collective-permute-done.21 = f32[96,256]{1,0:T(8,128)S(1)} collective-permute-done((f32[96,256]{1,0:T(8,128)S(1)}, f32[96,256]{1,0:T(8,128)S(1)}, u32[]{:S(2)}, u32[]{:S(2)}) %collective-permute-start.21) | collective-permute-done | bytes 98336 | tf_op jit(solution)/shard_map/ppermute | solution.py:35
  139.9 3.1 %collective-permute-start.23 = (f32[96,256]{1,0:T(8,128)S(1)}, f32[96,256]{1,0:T(8,128)S(1)}, u32[]{:S(2)}, u32[]{:S(2)}) collective-permute-start(f32[96,256]{1,0:T(8,128)S(1)} %add_add_fusion.mine_ref), channel_id=1, source_target_pairs={{0,8},{8,0},{16,24},{24,16},{32,40},{40,32},{48,56},{56,48},{64,72... | collective-permute-start | bytes 294920 | tf_op jit(solution)/shard_map/ppermute | solution.py:35
  143.9 9.5 %invert.1.inverse_ref = f32[256,256]{1,0:T(8,128)S(1)} custom-call(s32[4]{0:T(128)S(1)} %compare_select_fusion.2.meta, f32[96,256]{1,0:T(8,128)S(1)} %add_add_fusion.mine_ref, f32[96,256]{1,0:T(8,128)S(1)} %collective-permute-done.23.other_ref), custom_call_target="tpu_custom_call" | custom-call | tf_op jit(solution)/shard_map/invert/pallas_call | solution.py:359
  155.2 2.6 %coefs.1 = f32[256,2048]{1,0:T(8,128)} custom-call(s32[4]{0:T(128)S(1)} %compare_select_fusion.2.meta, f32[256,256]{1,0:T(8,128)S(1)} %invert.1.inverse_ref, bf16[128,2048]{1,0:T(8,128)(2,1)S(1)} %bitcast.12, bf16[128,2048]{1,0:T(8,128)(2,1)S(1)} %collective-permute-done.25.other_ref), custom_call_target="tpu_custom_call" | custom-call | tf_op jit(solution)/shard_map/coefs/pallas_call | solution.py:398
  (66 shorter events, 36.5 us)
Async XLA Ops:
  3.0 19.5 %all-to-all-start = ((bf16[8,64,256]{2,1,0:T(8,128)(2,1)}), bf16[8,64,256]{2,1,0:T(8,128)(2,1)S(1)}, u32[]{:S(2)}, u32[]{:S(2)}) async-start(bf16[8,64,256]{2,1,0:T(8,128)(2,1)} %bitcast.4), calls=%async_computation | async-start | bytes 524288 | tf_op jit(solution)/shard_map/all_to_all | solution.py:435
  23.9 9.0 %collective-permute-start.2 = (bf16[256,256]{1,0:T(8,128)(2,1)S(1)}, bf16[256,256]{1,0:T(8,128)(2,1)S(1)}, u32[]{:S(2)}, u32[]{:S(2)}) collective-permute-start(bf16[256,256]{1,0:T(8,128)(2,1)S(1)} %get-tuple-element.22), channel_id=1, source_target_pairs={{0,1},{1,2},{2,3},{3,4},{4,5},{5,6},{6,7},{7,0},{8,9},{9,10},{10,1... | collective-permute-start | bytes 393224 | tf_op jit(solution)/shard_map/ppermute | solution.py:31
  25.4 6.4 %collective-permute-start.3 = (bf16[128,256]{1,0:T(8,128)(2,1)S(1)}, bf16[128,256]{1,0:T(8,128)(2,1)S(1)}, u32[]{:S(2)}, u32[]{:S(2)}) collective-permute-start(bf16[128,256]{1,0:T(8,128)(2,1)S(1)} %get-tuple-element.23), channel_id=1, source_target_pairs={{0,2},{1,3},{2,4},{3,5},{4,6},{5,7},{6,0},{7,1},{8,10},{9,11},{10,... | collective-permute-start | bytes 196616 | tf_op jit(solution)/shard_map/ppermute | solution.py:31
  27.5 6.7 %collective-permute-start.6 = (bf16[128,256]{1,0:T(8,128)(2,1)S(1)}, bf16[128,256]{1,0:T(8,128)(2,1)S(1)}, u32[]{:S(2)}, u32[]{:S(2)}) collective-permute-start(bf16[128,256]{1,0:T(8,128)(2,1)S(1)} %get-tuple-element.26), channel_id=1, source_target_pairs={{0,6},{1,7},{2,0},{3,1},{4,2},{5,3},{6,4},{7,5},{8,14},{9,15},{10,... | collective-permute-start | bytes 196616 | tf_op jit(solution)/shard_map/ppermute | solution.py:31
  29.0 11.0 %collective-permute-start = (bf16[256,256]{1,0:T(8,128)(2,1)S(1)}, bf16[256,256]{1,0:T(8,128)(2,1)S(1)}, u32[]{:S(2)}, u32[]{:S(2)}) collective-permute-start(bf16[256,256]{1,0:T(8,128)(2,1)S(1)} %get-tuple-element.19), channel_id=1, source_target_pairs={{0,1},{1,2},{2,3},{3,4},{4,5},{5,6},{6,7},{7,0},{8,9},{9,10},{10,1... | collective-permute-start | bytes 393224 | tf_op jit(solution)/shard_map/ppermute | solution.py:31
  30.2 9.8 %collective-permute-start.1 = (bf16[256,256]{1,0:T(8,128)(2,1)S(1)}, bf16[256,256]{1,0:T(8,128)(2,1)S(1)}, u32[]{:S(2)}, u32[]{:S(2)}) collective-permute-start(bf16[256,256]{1,0:T(8,128)(2,1)S(1)} %get-tuple-element.20), channel_id=1, source_target_pairs={{0,7},{1,0},{2,1},{3,2},{4,3},{5,4},{6,5},{7,6},{8,15},{9,8},{10,9... | collective-permute-start | bytes 393224 | tf_op jit(solution)/shard_map/ppermute | solution.py:31
  31.8 6.7 %collective-permute-start.5 = (bf16[256,256]{1,0:T(8,128)(2,1)S(1)}, bf16[256,256]{1,0:T(8,128)(2,1)S(1)}, u32[]{:S(2)}, u32[]{:S(2)}) collective-permute-start(bf16[256,256]{1,0:T(8,128)(2,1)S(1)} %get-tuple-element.25), channel_id=1, source_target_pairs={{0,7},{1,0},{2,1},{3,2},{4,3},{5,4},{6,5},{7,6},{8,15},{9,8},{10,9... | collective-permute-start | bytes 393224 | tf_op jit(solution)/shard_map/ppermute | solution.py:31
  33.0 7.8 %collective-permute-start.4 = (bf16[256,256]{1,0:T(8,128)(2,1)S(1)}, bf16[256,256]{1,0:T(8,128)(2,1)S(1)}, u32[]{:S(2)}, u32[]{:S(2)}) collective-permute-start(bf16[256,256]{1,0:T(8,128)(2,1)S(1)} %add_convert_fusion.2), channel_id=1, source_target_pairs={{0,2},{1,3},{2,4},{3,5},{4,6},{5,7},{6,0},{7,1},{8,10},{9,11},{10,... | collective-permute-start | bytes 393224 | tf_op jit(solution)/shard_map/ppermute | solution.py:31
  38.5 8.0 %collective-permute-start.7 = (bf16[256,256]{1,0:T(8,128)(2,1)S(1)}, bf16[256,256]{1,0:T(8,128)(2,1)S(1)}, u32[]{:S(2)}, u32[]{:S(2)}) collective-permute-start(bf16[256,256]{1,0:T(8,128)(2,1)S(1)} %add_convert_fusion.1), channel_id=1, source_target_pairs={{0,6},{1,7},{2,0},{3,1},{4,2},{5,3},{6,4},{7,5},{8,14},{9,15},{10,... | collective-permute-start | bytes 393224 | tf_op jit(solution)/shard_map/ppermute | solution.py:31
  46.6 7.3 %collective-permute-start.11 = (bf16[256,256]{1,0:T(8,128)(2,1)S(1)}, bf16[256,256]{1,0:T(8,128)(2,1)S(1)}, u32[]{:S(2)}, u32[]{:S(2)}) collective-permute-start(bf16[256,256]{1,0:T(8,128)(2,1)S(1)} %add_convert_fusion.refs_0_), channel_id=1, source_target_pairs={{0,2},{1,3},{2,4},{3,5},{4,6},{5,7},{6,0},{7,1},{8,10},{9,11},{10,... | collective-permute-start | bytes 393224 | tf_op jit(solution)/shard_map/ppermute | solution.py:31
  48.3 5.6 %collective-permute-start.9 = (bf16[256,256]{1,0:T(8,128)(2,1)S(1)}, bf16[256,256]{1,0:T(8,128)(2,1)S(1)}, u32[]{:S(2)}, u32[]{:S(2)}) collective-permute-start(bf16[256,256]{1,0:T(8,128)(2,1)S(1)} %add_convert_fusion.refs_0_), channel_id=1, source_target_pairs={{0,6},{1,7},{2,0},{3,1},{4,2},{5,3},{6,4},{7,5},{8,14},{9,15},{10,... | collective-permute-start | bytes 393224 | tf_op jit(solution)/shard_map/ppermute | solution.py:31
  50.2 7.8 %collective-permute-start.15 = (bf16[256,256]{1,0:T(8,128)(2,1)S(1)}, bf16[256,256]{1,0:T(8,128)(2,1)S(1)}, u32[]{:S(2)}, u32[]{:S(2)}) collective-permute-start(bf16[256,256]{1,0:T(8,128)(2,1)S(1)} %add_convert_fusion.refs_0_), channel_id=1, source_target_pairs={{0,1},{1,2},{2,3},{3,4},{4,5},{5,6},{6,7},{7,0},{8,9},{9,10},{10,1... | collective-permute-start | bytes 393224 | tf_op jit(solution)/shard_map/ppermute | solution.py:31
  51.6 8.9 %collective-permute-start.8 = (bf16[256,256]{1,0:T(8,128)(2,1)S(1)}, bf16[256,256]{1,0:T(8,128)(2,1)S(1)}, u32[]{:S(2)}, u32[]{:S(2)}) collective-permute-start(bf16[256,256]{1,0:T(8,128)(2,1)S(1)} %add_convert_fusion.refs_0_), channel_id=1, source_target_pairs={{0,7},{1,0},{2,1},{3,2},{4,3},{5,4},{6,5},{7,6},{8,15},{9,8},{10,9... | collective-permute-start | bytes 393224 | tf_op jit(solution)/shard_map/ppermute | solution.py:31
  53.9 11.0 %collective-permute-start.14 = (bf16[256,256]{1,0:T(8,128)(2,1)S(1)}, bf16[256,256]{1,0:T(8,128)(2,1)S(1)}, u32[]{:S(2)}, u32[]{:S(2)}) collective-permute-start(bf16[256,256]{1,0:T(8,128)(2,1)S(1)} %collective-permute-done.11.refs_7_), channel_id=1, source_target_pairs={{0,1},{1,2},{2,3},{3,4},{4,5},{5,6},{6,7},{7,0},{8,9},{9,10},{10,1... | collective-permute-start | bytes 393224 | tf_op jit(solution)/shard_map/ppermute | solution.py:31
  53.9 11.0 %collective-permute-start.10 = (bf16[256,256]{1,0:T(8,128)(2,1)S(1)}, bf16[256,256]{1,0:T(8,128)(2,1)S(1)}, u32[]{:S(2)}, u32[]{:S(2)}) collective-permute-start(bf16[256,256]{1,0:T(8,128)(2,1)S(1)} %collective-permute-done.9.refs_2_), channel_id=1, source_target_pairs={{0,7},{1,0},{2,1},{3,2},{4,3},{5,4},{6,5},{7,6},{8,15},{9,8},{10,9... | collective-permute-start | bytes 393224 | tf_op jit(solution)/shard_map/ppermute | solution.py:31
  58.0 6.9 %collective-permute-start.13 = (bf16[128,256]{1,0:T(8,128)(2,1)S(1)}, bf16[128,256]{1,0:T(8,128)(2,1)S(1)}, u32[]{:S(2)}, u32[]{:S(2)}) collective-permute-start(bf16[128,256]{1,0:T(8,128)(2,1)S(1)} %slice.13), channel_id=1, source_target_pairs={{0,6},{1,7},{2,0},{3,1},{4,2},{5,3},{6,4},{7,5},{8,14},{9,15},{10,... | collective-permute-start | bytes 196616 | tf_op jit(solution)/shard_map/ppermute | solution.py:31
  73.1 8.1 %collective-permute-start.24 = (bf16[128,2176]{1,0:T(8,128)(2,1)S(1)}, bf16[128,2176]{1,0:T(8,128)(2,1)S(1)}, u32[]{:S(2)}, u32[]{:S(2)}) collective-permute-start(bf16[128,2176]{1,0:T(8,128)(2,1)S(1)} %get-tuple-element.31), channel_id=1, source_target_pairs={{0,8},{8,0},{16,24},{24,16},{32,40},{40,32},{48,56},{56,48},{64,72... | collective-permute-start | bytes 1671176 | tf_op jit(solution)/shard_map/ppermute | solution.py:35
  113.7 12.5 %all-to-all-start.3 = ((bf16[16,8,2048]{2,1,0:T(8,128)(2,1)}), bf16[16,8,2048]{2,1,0:T(8,128)(2,1)S(1)}, u32[]{:S(2)}, u32[]{:S(2)}) async-start(bf16[16,8,2048]{2,1,0:T(8,128)(2,1)} %insert.1), calls=%async_computation.3 | async-start | bytes 1048576 | tf_op jit(solution)/shard_map/all_to_all | solution.py:410
  121.6 9.8 %collective-permute-start.19 = (f32[96,256]{1,0:T(8,128)S(1)}, f32[96,256]{1,0:T(8,128)S(1)}, u32[]{:S(2)}, u32[]{:S(2)}) collective-permute-start(f32[96,256]{1,0:T(8,128)S(1)} %add.61), channel_id=1, source_target_pairs={{0,48},{8,56},{16,0},{24,8},{32,16},{40,24},{48,32},{56,40},{64,11... | collective-permute-start | bytes 294920 | tf_op jit(solution)/shard_map/ppermute | solution.py:35
  124.3 7.1 %collective-permute-start.18 = (f32[96,256]{1,0:T(8,128)S(1)}, f32[96,256]{1,0:T(8,128)S(1)}, u32[]{:S(2)}, u32[]{:S(2)}) collective-permute-start(f32[96,256]{1,0:T(8,128)S(1)} %add.61), channel_id=1, source_target_pairs={{0,16},{8,24},{16,32},{24,40},{32,48},{40,56},{48,0},{56,8},{64,80... | collective-permute-start | bytes 294920 | tf_op jit(solution)/shard_map/ppermute | solution.py:35
  124.3 7.2 %collective-permute-start.17 = (f32[96,256]{1,0:T(8,128)S(1)}, f32[96,256]{1,0:T(8,128)S(1)}, u32[]{:S(2)}, u32[]{:S(2)}) collective-permute-start(f32[96,256]{1,0:T(8,128)S(1)} %add.61), channel_id=1, source_target_pairs={{0,32},{8,40},{16,48},{24,56},{32,0},{40,8},{48,16},{56,24},{64,96... | collective-permute-start | bytes 294920 | tf_op jit(solution)/shard_map/ppermute | solution.py:35
  126.3 28.9 %collective-permute-start.25 = (bf16[128,2048]{1,0:T(8,128)(2,1)S(1)}, bf16[128,2048]{1,0:T(8,128)(2,1)S(1)}, u32[]{:S(2)}, u32[]{:S(2)}) collective-permute-start(bf16[128,2048]{1,0:T(8,128)(2,1)S(1)} %bitcast.11), channel_id=1, source_target_pairs={{0,8},{8,0},{16,24},{24,16},{32,40},{40,32},{48,56},{56,48},{64,72... | collective-permute-start | bytes 1572872 | tf_op jit(solution)/shard_map/ppermute | solution.py:35
  134.1 5.7 %collective-permute-start.21 = (f32[96,256]{1,0:T(8,128)S(1)}, f32[96,256]{1,0:T(8,128)S(1)}, u32[]{:S(2)}, u32[]{:S(2)}) collective-permute-start(f32[96,256]{1,0:T(8,128)S(1)} %add_add_fusion.1), channel_id=1, source_target_pairs={{0,64},{8,72},{16,80},{24,88},{32,96},{40,104},{48,112},{56,120},{... | collective-permute-start | bytes 294920 | tf_op jit(solution)/shard_map/ppermute | solution.py:35
  134.1 5.7 %collective-permute-start.20 = (f32[96,256]{1,0:T(8,128)S(1)}, f32[96,256]{1,0:T(8,128)S(1)}, u32[]{:S(2)}, u32[]{:S(2)}) collective-permute-start(f32[96,256]{1,0:T(8,128)S(1)} %add_add_fusion.1), channel_id=1, source_target_pairs={{0,128},{8,136},{16,144},{24,152},{32,160},{40,168},{48,176},{56,1... | collective-permute-start | bytes 294920 | tf_op jit(solution)/shard_map/ppermute | solution.py:35
  (10 other events, 72.4 us)
